TPU v7x, 128 devices: a whole 4x4x4 slice. The times are simulated.
128 devices in a mesh: section: 8 (over x, core), seq: 16 (over z, y).
Axes of the slice: x: 4, y: 4, z: 4, core: 2. Of those that a mesh axis runs over, the one named last changes fastest.
Arguments:
- residual: bfloat16 [8, 4096, 2048], P('section', 'seq'), may hold values from -6 to 6
- w_qkv: bfloat16 [8, 2048, 6144], P('section', 'seq'), may hold values from -0.125 to 0.125
- w_beta: bfloat16 [8, 2048, 16], P('section', 'seq'), may hold values from -0.125 to 0.125
- beta_bias: float32 [8, 16], P('section'), may hold values from -8 to 2
- norm_gain: float32 [8, 2048], P('section'), may hold values from 0.1 to 1.9
- out_gain: float32 [8, 128], P('section'), may hold values from 0.1 to 1.9
- state_in: float32 [8, 16, 128, 128], P('section'), may hold values from -6 to 6
- doc_start: int32 [2, 8], P(None, 'section'), may hold values from 0 to 64, as said below
Outputs:
- stream_out: bfloat16 [8, 4096, 2048], P('section', 'seq')
Inputs may be any that keep to these rules, and one draw needn't show every extreme that they name: `doc_start`: 64 means no new document in that micro-batch.
All inputs are finite; a program needn't handle non-finite values.
Results may differ from a plain program's by a relative error of at most 0.03.
Values may be sent and summed in bfloat16 or wider, within the bound.
No kernel may reach another device: no remote copies, remote signals or barrier semaphores. Data moves between devices by JAX's collectives and lax.ppermute only.
A program may use at most 192 MiB of HBM per device.

v0:
```python
import jax
import jax.numpy as jnp
from jax import lax
from jax.sharding import PartitionSpec as P

HEADS = 16
HD = 128
GROUP = 64
TICKS = 2
FULL_PRECISION = lax.Precision.HIGHEST


def from_behind(value, axis, by):
    count = lax.axis_size(axis)
    pairs = [(i, i + by) for i in range(count) if 0 <= i + by < count]
    return lax.ppermute(value, axis, pairs)


def from_root(value, axis, source):
    kept = jnp.where(lax.axis_index(axis) == source, value, 0).astype(value.dtype)
    return lax.psum(kept, axis)


def passed_along(value, axis, by):
    count = lax.axis_size(axis)
    return lax.ppermute(value, axis, [(i, (i + by) % count) for i in range(count)])


def unit_norm(projected):
    return projected * lax.rsqrt(jnp.sum(projected * projected, axis=-1, keepdims=True) + 1e-06)


def block_solve(key_rows, values, beta_rows):
    block_len = key_rows.shape[-2]
    intersections = jnp.einsum("ghik,ghjk->ghij", key_rows, key_rows, precision=FULL_PRECISION)
    system = jnp.tril(intersections * beta_rows[..., :, None], -1) + jnp.eye(
        block_len, dtype=jnp.float32
    )
    right_side = jnp.concatenate(
        [values * beta_rows[..., None], key_rows * beta_rows[..., None]], axis=-1
    )
    solved = lax.linalg.triangular_solve(
        system, right_side, left_side=True, lower=True, unit_diagonal=True
    )
    head_width = values.shape[-1]
    return (solved[..., :head_width], solved[..., head_width:])


def prepare(stream, weight_qkv, weight_beta, head_bias, in_gain):
    row_count = stream.shape[0]
    widened = stream.astype(jnp.float32)
    normed = (
        widened * lax.rsqrt(jnp.mean(widened * widened, axis=-1, keepdims=True) + 1e-05) * in_gain
    ).astype(jnp.bfloat16)
    projected = jnp.dot(normed, weight_qkv, preferred_element_type=jnp.float32).reshape(
        row_count, 3, HEADS, HD
    )
    queries = unit_norm(projected[:, 0]).astype(jnp.bfloat16)
    key_rows = unit_norm(projected[:, 1]).astype(jnp.bfloat16)
    values = projected[:, 2].astype(jnp.bfloat16)
    beta_rows = jax.nn.sigmoid(
        jnp.dot(normed, weight_beta, preferred_element_type=jnp.float32) + head_bias
    )
    blocks = row_count // GROUP

    def to_blocks(tensor):
        return tensor.astype(jnp.float32).reshape(blocks, GROUP, HEADS, HD).transpose(0, 2, 1, 3)

    beta_blk = beta_rows.reshape(blocks, GROUP, HEADS).transpose(0, 2, 1)
    key_block = to_blocks(key_rows)
    inject, weights = block_solve(key_block, to_blocks(values), beta_blk)
    return (to_blocks(queries), key_block, inject, weights, widened)


def run_blocks(queries, key_rows, inject, weights, current_state, doc_block, first_block):
    block_count = queries.shape[0]
    block_len = queries.shape[2]
    causal = jnp.tril(jnp.ones((block_len, block_len), jnp.float32))

    def run_advance(current_state, pieces):
        query_block, key_block, inject_block, weight_block, block_index = pieces
        current_state = jnp.where(
            block_index == doc_block, jnp.zeros_like(current_state), current_state
        )
        delta_values = inject_block - jnp.einsum(
            "jxy,jyu->jxu", weight_block, current_state, precision=FULL_PRECISION
        )
        attention_scores = (
            jnp.einsum("hik,hjk->hij", query_block, key_block, precision=FULL_PRECISION) * causal
        )
        block_result = jnp.einsum(
            "jxy,jyu->jxu", query_block, current_state, precision=FULL_PRECISION
        ) + jnp.einsum("ucd,udo->uco", attention_scores, delta_values, precision=FULL_PRECISION)
        current_state = current_state + jnp.einsum(
            "plq,plw->pqw", key_block, delta_values, precision=FULL_PRECISION
        )
        return (current_state, block_result)

    block_ids = first_block + jnp.arange(block_count, dtype=jnp.int32)
    return lax.scan(run_advance, current_state, (queries, key_rows, inject, weights, block_ids))


def transitions(key_rows, inject, weights, doc_block, first_block):
    head_count = key_rows.shape[1]
    head_width = key_rows.shape[3]
    block_count = key_rows.shape[0]
    identity = jnp.broadcast_to(
        jnp.eye(head_width, dtype=jnp.float32), (head_count, head_width, head_width)
    )

    def transitions_advance(maps, pieces):
        decay_matrix, start_offset = maps
        key_block, inject_block, weight_block, block_index = pieces
        keep_flag = block_index != doc_block
        decay_matrix = jnp.where(keep_flag, decay_matrix, jnp.zeros_like(decay_matrix))
        start_offset = jnp.where(keep_flag, start_offset, jnp.zeros_like(start_offset))
        decay_matrix = decay_matrix - jnp.einsum(
            "plq,plw->pqw",
            key_block,
            jnp.einsum("jxy,jyu->jxu", weight_block, decay_matrix, precision=FULL_PRECISION),
            precision=FULL_PRECISION,
        )
        start_offset = start_offset + jnp.einsum(
            "plq,plw->pqw",
            key_block,
            inject_block
            - jnp.einsum("jxy,jyu->jxu", weight_block, start_offset, precision=FULL_PRECISION),
            precision=FULL_PRECISION,
        )
        return ((decay_matrix, start_offset), None)

    block_ids = first_block + jnp.arange(block_count, dtype=jnp.int32)
    maps, unused = lax.scan(
        transitions_advance,
        (identity, jnp.zeros_like(identity)),
        (key_rows, inject, weights, block_ids),
    )
    return maps


def apply_map(maps, given_state):
    return jnp.einsum("hij,hjk->hik", maps[0], given_state, precision=FULL_PRECISION) + maps[1]


def compose(earlier, latter):
    return (
        jnp.einsum("hij,hjk->hik", latter[0], earlier[0], precision=FULL_PRECISION),
        jnp.einsum("hij,hjk->hik", latter[0], earlier[1], precision=FULL_PRECISION) + latter[1],
    )


def finish(widened, block_result, head_gain):
    blocks = block_result.shape[0]
    mixed = block_result.transpose(0, 2, 1, 3).reshape(blocks * GROUP, HEADS, HD)
    mixed = mixed * lax.rsqrt(jnp.mean(mixed * mixed, axis=-1, keepdims=True) + 1e-05) * head_gain
    return (widened + mixed.reshape(blocks * GROUP, HEADS * HD)).astype(jnp.bfloat16)


def shards(residual, w_qkv, w_beta, beta_bias, norm_gain, out_gain, state_in, doc_start):
    weight_qkv, weight_beta = (
        lax.all_gather(w_qkv[0], "seq", axis=0, tiled=True),
        lax.all_gather(w_beta[0], "seq", axis=0, tiled=True),
    )
    seq_count = lax.axis_size("seq")
    position = lax.axis_index("seq")
    stream = residual[0]
    given_state = state_in[0]
    blocks = stream.shape[0] // GROUP
    first_block = position * blocks
    outputs = stream
    identity = jnp.broadcast_to(jnp.eye(HD, dtype=jnp.float32), (HEADS, HD, HD))
    empty_map = jnp.stack([identity, jnp.zeros_like(identity)])
    for tick_index in range(TICKS):
        doc_block = doc_start[tick_index, 0]
        queries, key_rows, inject, weights, widened = prepare(
            stream, weight_qkv, weight_beta, beta_bias[0], norm_gain[0]
        )
        maps = transitions(key_rows, inject, weights, doc_block, first_block)

        def hop_once(hop_index, carried_map):
            joined = compose((carried_map[0], carried_map[1]), maps)
            passed = from_behind(
                jnp.stack([joined[0], joined[1]]).astype(jnp.bfloat16), "seq", 1
            ).astype(jnp.float32)
            return jnp.where(position == 0, empty_map, passed)

        prefix_map = lax.fori_loop(0, seq_count - 1, hop_once, empty_map)
        prefix = (prefix_map[0], prefix_map[1])
        entry_state = apply_map(prefix, given_state)
        final_state, block_result = run_blocks(
            queries, key_rows, inject, weights, entry_state, doc_block, first_block
        )
        outputs = finish(widened, block_result, out_gain[0])
        if tick_index + 1 < TICKS:
            given_state = from_root(final_state.astype(jnp.bfloat16), "seq", seq_count - 1).astype(
                final_state.dtype
            )
            stream = passed_along(outputs, "section", 1)
    return outputs[None]


def solution(mesh):
    return jax.shard_map(
        shards,
        mesh=mesh,
        in_specs=(
            P("section", "seq", None),
            P("section", "seq", None),
            P("section", "seq", None),
            P("section", None),
            P("section", None),
            P("section", None),
            P("section", None, None, None),
            P(None, "section"),
        ),
        out_specs=P("section", "seq", None),
        check_vma=False,
    )
```

profile of v0, /device:TPU:34, one launch (start us, length us, event | category | flops | bytes accessed | tf_op | source)
XLA Modules:
  0.0 2081.2 jit_solution(3336317457587673220)
XLA Ops:
  7.3 24.4 %all-gather.1 = bf16[1,2048,16]{1,2,0:T(8,128)(2,1)S(1)} all-gather(bf16[1,128,16]{1,2,0:T(8,128)(2,1)} %param.24), channel_id=3, replica_groups=mesh['section'=8,'seq'=16] {'seq'}, dimensions={1}, use_global_device_ids=true | all-gather | bytes 69632 | tf_op jit(solution)/shard_map/all_gather | solution.py:162
  35.8 130.0 %all-gather.4.cloned.1.call-done = bf16[1,2048,6144]{2,1,0:T(8,128)(2,1)} async-done(((bf16[1,128,6144]{2,1,0:T(8,128)(2,1)}), bf16[1,2048,6144]{2,1,0:T(8,128)(2,1)}) %all-gather.4.cloned.1.call-update) | async-done | bytes 25165840 | tf_op jit(solution)/shard_map/all_gather | solution.py:161
  165.8 29.7 %copy.95 = bf16[6144,2048]{1,0:T(8,128)(2,1)} copy(bf16[6144,2048]{0,1:T(8,128)(2,1)} %bitcast.357) | data formatting | bytes 50331648 | tf_op jit(solution)/shard_map/dot_general | solution.py:55
  195.5 11.4 fusion.150
  209.8 4.0 broadcast_multiply_fusion.1
  217.8 316.0 %custom-call.6 = f32[4,16,1,64,64]{3,4,2,1,0:T(8,128)} custom-call(f32[4,16,1,64,64]{4,3,2,1,0:T(8,128)} %add_bitcast_fusion.1), custom_call_target="InvertDiagBlocksLowerTriangular" | custom-call | tf_op jit(solution)/shard_map/triangular_solve/custom-call.1 | solution.py:42
  533.8 6.6 fusion.107
  543.2 41.3 %while.80 = (s32[]{:T(128)}, f32[16,128,128]{2,1,0:T(8,128)S(1)}, f32[16,128,128]{2,1,0:T(8,128)S(1)}, s32[4]{0:T(128)S(1)}, s32[]{:T(128)}, /*index=5*/f32[4,16...) while((s32[]{:T(128)}, f32[16,128,128]{2,1,0:T(8,128)S(1)}, ...), condition=%wide.region_3.5_spmd.clone, body=%wide.region_2.4_spmd.clone.sunk | while | flops 807534592 | bytes 19400364 | solution.py:133
  584.6 464.3 %while.76 = (s32[]{:T(128)}, f32[2,16,128,128]{3,2,1,0:T(8,128)}, pred[]{:T(512)}, f32[16,128,128]{2,1,0:T(8,128)S(1)}, f32[16,128,128]{2,1,0:T(8,128)S(1)}, /*index=5*/f32[2,16,128,128]{3,2,1,0:T(8,128)}, s32[]{:T(128)}) while((s32[]{:T(128)}, f32[2,16,128,128]{3,2,1,0:T(8,128)}, pred[]{:T(512)}, f32[16,128,128]{2,1,0:T(8,128)S(1)}, ...), condition=%wide.region_5.7_spmd, body=%wide.region_4.6_spmd.sunk | while | flops 807665664 | bytes 26214544 | solution.py:187
  591.6 27.0 %collective-permute-done = bf16[2,16,128,128]{3,2,1,0:T(8,128)(2,1)} collective-permute-done((bf16[2,16,128,128]{3,2,1,0:T(8,128)(2,1)}, bf16[2,16,128,128]{3,2,1,0:T(8,128)(2,1)}, u32[]{:S(2)}, u32[]{:S(2)}) %collective-permute-start) | collective-permute-done | bytes 1048608 | tf_op jit(solution)/shard_map/while/body/eval_jaxpr/ppermute | solution.py:16
  628.4 26.4 %collective-permute-done = bf16[2,16,128,128]{3,2,1,0:T(8,128)(2,1)} collective-permute-done((bf16[2,16,128,128]{3,2,1,0:T(8,128)(2,1)}, bf16[2,16,128,128]{3,2,1,0:T(8,128)(2,1)}, u32[]{:S(2)}, u32[]{:S(2)}) %collective-permute-start) | collective-permute-done | bytes 1048608 | tf_op jit(solution)/shard_map/while/body/eval_jaxpr/ppermute | solution.py:16
  664.5 25.5 %collective-permute-done = bf16[2,16,128,128]{3,2,1,0:T(8,128)(2,1)} collective-permute-done((bf16[2,16,128,128]{3,2,1,0:T(8,128)(2,1)}, bf16[2,16,128,128]{3,2,1,0:T(8,128)(2,1)}, u32[]{:S(2)}, u32[]{:S(2)}) %collective-permute-start) | collective-permute-done | bytes 1048608 | tf_op jit(solution)/shard_map/while/body/eval_jaxpr/ppermute | solution.py:16
  699.7 24.6 %collective-permute-done = bf16[2,16,128,128]{3,2,1,0:T(8,128)(2,1)} collective-permute-done((bf16[2,16,128,128]{3,2,1,0:T(8,128)(2,1)}, bf16[2,16,128,128]{3,2,1,0:T(8,128)(2,1)}, u32[]{:S(2)}, u32[]{:S(2)}) %collective-permute-start) | collective-permute-done | bytes 1048608 | tf_op jit(solution)/shard_map/while/body/eval_jaxpr/ppermute | solution.py:16
  734.0 23.6 %collective-permute-done = bf16[2,16,128,128]{3,2,1,0:T(8,128)(2,1)} collective-permute-done((bf16[2,16,128,128]{3,2,1,0:T(8,128)(2,1)}, bf16[2,16,128,128]{3,2,1,0:T(8,128)(2,1)}, u32[]{:S(2)}, u32[]{:S(2)}) %collective-permute-start) | collective-permute-done | bytes 1048608 | tf_op jit(solution)/shard_map/while/body/eval_jaxpr/ppermute | solution.py:16
  767.3 22.7 %collective-permute-done = bf16[2,16,128,128]{3,2,1,0:T(8,128)(2,1)} collective-permute-done((bf16[2,16,128,128]{3,2,1,0:T(8,128)(2,1)}, bf16[2,16,128,128]{3,2,1,0:T(8,128)(2,1)}, u32[]{:S(2)}, u32[]{:S(2)}) %collective-permute-start) | collective-permute-done | bytes 1048608 | tf_op jit(solution)/shard_map/while/body/eval_jaxpr/ppermute | solution.py:16
  799.8 21.8 %collective-permute-done = bf16[2,16,128,128]{3,2,1,0:T(8,128)(2,1)} collective-permute-done((bf16[2,16,128,128]{3,2,1,0:T(8,128)(2,1)}, bf16[2,16,128,128]{3,2,1,0:T(8,128)(2,1)}, u32[]{:S(2)}, u32[]{:S(2)}) %collective-permute-start) | collective-permute-done | bytes 1048608 | tf_op jit(solution)/shard_map/while/body/eval_jaxpr/ppermute | solution.py:16
  831.3 20.9 %collective-permute-done = bf16[2,16,128,128]{3,2,1,0:T(8,128)(2,1)} collective-permute-done((bf16[2,16,128,128]{3,2,1,0:T(8,128)(2,1)}, bf16[2,16,128,128]{3,2,1,0:T(8,128)(2,1)}, u32[]{:S(2)}, u32[]{:S(2)}) %collective-permute-start) | collective-permute-done | bytes 1048608 | tf_op jit(solution)/shard_map/while/body/eval_jaxpr/ppermute | solution.py:16
  861.8 20.0 collective-permute-done
  891.5 19.0 collective-permute-done
  920.2 18.1 collective-permute-done
  948.1 17.2 collective-permute-done
  975.0 17.2 collective-permute-done
  1001.9 17.2 collective-permute-done
  1028.7 17.2 collective-permute-done
  1055.1 48.0 %while.78 = (s32[]{:T(128)}, f32[16,128,128]{2,1,0:T(8,128)S(1)}, f32[4,16,64,128]{3,2,1,0:T(8,128)}, s32[4]{0:T(128)S(1)}, s32[]{:T(128)}, /*index=5*/f32[4,16,...) while((s32[]{:T(128)}, f32[16,128,128]{2,1,0:T(8,128)S(1)}, ...), condition=%wide.region_8.10_spmd.clone, body=%wide.region_7.9_spmd.clone.sunk | while | flops 806690816 | bytes 19451036 | solution.py:100
  1115.3 11.7 collective-permute-done.2
  1128.5 12.3 fusion.115
  1150.9 5.2 broadcast_multiply_fusion
  1161.5 316.2 %custom-call.7 = f32[4,16,1,64,64]{3,4,2,1,0:T(8,128)} custom-call(f32[4,16,1,64,64]{4,3,2,1,0:T(8,128)} %add_bitcast_fusion), custom_call_target="InvertDiagBlocksLowerTriangular" | custom-call | tf_op jit(solution)/shard_map/triangular_solve/custom-call.1 | solution.py:42
  1477.7 6.6 fusion.111
  1487.0 54.6 %while.81 = (s32[]{:T(128)}, f32[16,128,128]{2,1,0:T(8,128)S(1)}, f32[16,128,128]{2,1,0:T(8,128)}, s32[4]{0:T(128)S(1)}, s32[]{:T(128)}, /*index=5*/f32[4,16,64,...) while((s32[]{:T(128)}, f32[16,128,128]{2,1,0:T(8,128)S(1)}, ...), condition=%wide.region_13.15_spmd.clone, body=%wide.region_12.14_spmd.clone.sunk | while | flops 807534592 | bytes 19401408 | solution.py:133
  1545.3 471.8 %while.77 = (s32[]{:T(128)}, f32[2,16,128,128]{3,2,1,0:T(8,128)}, pred[]{:T(512)}, f32[16,128,128]{2,1,0:T(8,128)S(1)}, f32[16,128,128]{2,1,0:T(8,128)}, /*index=5*/f32[2,16,128,128]{3,2,1,0:T(8,128)S(1)}, s32[]{:T(128)}) while((s32[]{:T(128)}, f32[2,16,128,128]{3,2,1,0:T(8,128)}, pred[]{:T(512)}, f32[16,128,128]{2,1,0:T(8,128)S(1)}, ...), condition=%wide.region_15.17_spmd, body=%wide.region_14.16_spmd.sunk | while | flops 807665664 | bytes 22020240 | solution.py:187
  1553.4 26.6 %collective-permute-done.1 = bf16[2,16,128,128]{3,2,1,0:T(8,128)(2,1)} collective-permute-done((bf16[2,16,128,128]{3,2,1,0:T(8,128)(2,1)}, bf16[2,16,128,128]{3,2,1,0:T(8,128)(2,1)}, u32[]{:S(2)}, u32[]{:S(2)}) %collective-permute-start.1) | collective-permute-done | bytes 1048608 | tf_op jit(solution)/shard_map/while/body/eval_jaxpr/ppermute | solution.py:16
  1590.7 25.7 %collective-permute-done.1 = bf16[2,16,128,128]{3,2,1,0:T(8,128)(2,1)} collective-permute-done((bf16[2,16,128,128]{3,2,1,0:T(8,128)(2,1)}, bf16[2,16,128,128]{3,2,1,0:T(8,128)(2,1)}, u32[]{:S(2)}, u32[]{:S(2)}) %collective-permute-start.1) | collective-permute-done | bytes 1048608 | tf_op jit(solution)/shard_map/while/body/eval_jaxpr/ppermute | solution.py:16
  1627.1 24.8 %collective-permute-done.1 = bf16[2,16,128,128]{3,2,1,0:T(8,128)(2,1)} collective-permute-done((bf16[2,16,128,128]{3,2,1,0:T(8,128)(2,1)}, bf16[2,16,128,128]{3,2,1,0:T(8,128)(2,1)}, u32[]{:S(2)}, u32[]{:S(2)}) %collective-permute-start.1) | collective-permute-done | bytes 1048608 | tf_op jit(solution)/shard_map/while/body/eval_jaxpr/ppermute | solution.py:16
  1662.6 23.8 %collective-permute-done.1 = bf16[2,16,128,128]{3,2,1,0:T(8,128)(2,1)} collective-permute-done((bf16[2,16,128,128]{3,2,1,0:T(8,128)(2,1)}, bf16[2,16,128,128]{3,2,1,0:T(8,128)(2,1)}, u32[]{:S(2)}, u32[]{:S(2)}) %collective-permute-start.1) | collective-permute-done | bytes 1048608 | tf_op jit(solution)/shard_map/while/body/eval_jaxpr/ppermute | solution.py:16
  1697.2 22.9 %collective-permute-done.1 = bf16[2,16,128,128]{3,2,1,0:T(8,128)(2,1)} collective-permute-done((bf16[2,16,128,128]{3,2,1,0:T(8,128)(2,1)}, bf16[2,16,128,128]{3,2,1,0:T(8,128)(2,1)}, u32[]{:S(2)}, u32[]{:S(2)}) %collective-permute-start.1) | collective-permute-done | bytes 1048608 | tf_op jit(solution)/shard_map/while/body/eval_jaxpr/ppermute | solution.py:16
  1730.8 22.0 %collective-permute-done.1 = bf16[2,16,128,128]{3,2,1,0:T(8,128)(2,1)} collective-permute-done((bf16[2,16,128,128]{3,2,1,0:T(8,128)(2,1)}, bf16[2,16,128,128]{3,2,1,0:T(8,128)(2,1)}, u32[]{:S(2)}, u32[]{:S(2)}) %collective-permute-start.1) | collective-permute-done | bytes 1048608 | tf_op jit(solution)/shard_map/while/body/eval_jaxpr/ppermute | solution.py:16
  1763.6 21.1 %collective-permute-done.1 = bf16[2,16,128,128]{3,2,1,0:T(8,128)(2,1)} collective-permute-done((bf16[2,16,128,128]{3,2,1,0:T(8,128)(2,1)}, bf16[2,16,128,128]{3,2,1,0:T(8,128)(2,1)}, u32[]{:S(2)}, u32[]{:S(2)}) %collective-permute-start.1) | collective-permute-done | bytes 1048608 | tf_op jit(solution)/shard_map/while/body/eval_jaxpr/ppermute | solution.py:16
  1795.3 20.1 collective-permute-done.1
  1826.2 19.2 collective-permute-done.1
  1856.2 18.3 collective-permute-done.1
  1885.2 17.4 collective-permute-done.1
  1913.3 17.2 collective-permute-done.1
  1941.2 17.2 collective-permute-done.1
  1969.2 17.2 collective-permute-done.1
  1997.1 17.2 collective-permute-done.1
  2021.2 44.4 %while.79 = (s32[]{:T(128)}, f32[16,128,128]{2,1,0:T(8,128)S(1)}, f32[4,16,64,128]{3,2,1,0:T(8,128)}, s32[4]{0:T(128)S(1)}, s32[]{:T(128)}, /*index=5*/f32[4,16,...) while((s32[]{:T(128)}, f32[16,128,128]{2,1,0:T(8,128)S(1)}, ...), condition=%wide.region_19.21_spmd.clone, body=%wide.region_18.20_spmd.clone.sunk | while | flops 806690816 | bytes 12109449 | solution.py:100
  (453 shorter events, 539.9 us)
Async XLA Ops:
  6.5 1042.4 %copy-start = (f32[1,16,128,128]{3,2,1,0:T(8,128)S(1)}, f32[1,16,128,128]{3,2,1,0:T(8,128)}, u32[]{:S(2)}) copy-start(f32[1,16,128,128]{3,2,1,0:T(8,128)} %param.28) | copy-start | bytes 3145732
  6.5 25.2 %copy-start.17 = (bf16[1,256,2048]{2,1,0:T(8,128)(2,1)S(1)}, bf16[1,256,2048]{2,1,0:T(8,128)(2,1)}, u32[]{:S(2)}) copy-start(bf16[1,256,2048]{2,1,0:T(8,128)(2,1)} %param.22) | copy-start | bytes 3145732
  6.5 25.5 %copy-start.21 = (f32[1,2048]{1,0:T(1,128)S(1)}, f32[1,2048]{1,0:T(1,128)}, u32[]{:S(2)}) copy-start(f32[1,2048]{1,0:T(1,128)} %param.26) | copy-start | bytes 24580
  6.5 25.5 %copy-start.22 = (f32[1,16]{1,0:T(1,128)S(1)}, f32[1,16]{1,0:T(1,128)}, u32[]{:S(2)}) copy-start(f32[1,16]{1,0:T(1,128)} %param.25) | copy-start | bytes 196
  6.5 159.2 %all-gather.4.cloned.1.call-start = ((), (), s32[]{:S(2)}) async-start(), calls=%async_computation.1 | async-start | bytes 26738688 | tf_op jit(solution)/shard_map/all_gather | solution.py:161
  7.3 1538.0 %all-reduce.3.cloned.1.call-start = ((), (), s32[]{:S(2)}) async-start(), calls=%async_computation | async-start | bytes 1048576 | tf_op jit(solution)/shard_map/psum | solution.py:21
  33.0 2.7 copy-start.20
  584.6 2.5 copy-start.9
  589.4 29.2 %collective-permute-start = (bf16[2,16,128,128]{3,2,1,0:T(8,128)(2,1)}, bf16[2,16,128,128]{3,2,1,0:T(8,128)(2,1)}, u32[]{:S(2)}, u32[]{:S(2)}) collective-permute-start(bf16[2,16,128,128]{3,2,1,0:T(8,128)(2,1)} %pad_maximum_fusion.4), channel_id=1, source_target_pairs={{0,1},{1,2},{2,3},{3,4},{4,5},{5,6},{6,7},{7,8},{8,9},{9,10},{10,1... | collective-permute-start | bytes 3145736 | tf_op jit(solution)/shard_map/while/body/eval_jaxpr/ppermute | solution.py:16
  626.4 28.3 %collective-permute-start = (bf16[2,16,128,128]{3,2,1,0:T(8,128)(2,1)}, bf16[2,16,128,128]{3,2,1,0:T(8,128)(2,1)}, u32[]{:S(2)}, u32[]{:S(2)}) collective-permute-start(bf16[2,16,128,128]{3,2,1,0:T(8,128)(2,1)} %pad_maximum_fusion.4), channel_id=1, source_target_pairs={{0,1},{1,2},{2,3},{3,4},{4,5},{5,6},{6,7},{7,8},{8,9},{9,10},{10,1... | collective-permute-start | bytes 3145736 | tf_op jit(solution)/shard_map/while/body/eval_jaxpr/ppermute | solution.py:16
  662.6 27.4 %collective-permute-start = (bf16[2,16,128,128]{3,2,1,0:T(8,128)(2,1)}, bf16[2,16,128,128]{3,2,1,0:T(8,128)(2,1)}, u32[]{:S(2)}, u32[]{:S(2)}) collective-permute-start(bf16[2,16,128,128]{3,2,1,0:T(8,128)(2,1)} %pad_maximum_fusion.4), channel_id=1, source_target_pairs={{0,1},{1,2},{2,3},{3,4},{4,5},{5,6},{6,7},{7,8},{8,9},{9,10},{10,1... | collective-permute-start | bytes 3145736 | tf_op jit(solution)/shard_map/while/body/eval_jaxpr/ppermute | solution.py:16
  697.8 26.5 %collective-permute-start = (bf16[2,16,128,128]{3,2,1,0:T(8,128)(2,1)}, bf16[2,16,128,128]{3,2,1,0:T(8,128)(2,1)}, u32[]{:S(2)}, u32[]{:S(2)}) collective-permute-start(bf16[2,16,128,128]{3,2,1,0:T(8,128)(2,1)} %pad_maximum_fusion.4), channel_id=1, source_target_pairs={{0,1},{1,2},{2,3},{3,4},{4,5},{5,6},{6,7},{7,8},{8,9},{9,10},{10,1... | collective-permute-start | bytes 3145736 | tf_op jit(solution)/shard_map/while/body/eval_jaxpr/ppermute | solution.py:16
  727.2 2.5 copy-start.9
  732.0 25.6 %collective-permute-start = (bf16[2,16,128,128]{3,2,1,0:T(8,128)(2,1)}, bf16[2,16,128,128]{3,2,1,0:T(8,128)(2,1)}, u32[]{:S(2)}, u32[]{:S(2)}) collective-permute-start(bf16[2,16,128,128]{3,2,1,0:T(8,128)(2,1)} %pad_maximum_fusion.4), channel_id=1, source_target_pairs={{0,1},{1,2},{2,3},{3,4},{4,5},{5,6},{6,7},{7,8},{8,9},{9,10},{10,1... | collective-permute-start | bytes 3145736 | tf_op jit(solution)/shard_map/while/body/eval_jaxpr/ppermute | solution.py:16
  765.4 24.6 %collective-permute-start = (bf16[2,16,128,128]{3,2,1,0:T(8,128)(2,1)}, bf16[2,16,128,128]{3,2,1,0:T(8,128)(2,1)}, u32[]{:S(2)}, u32[]{:S(2)}) collective-permute-start(bf16[2,16,128,128]{3,2,1,0:T(8,128)(2,1)} %pad_maximum_fusion.4), channel_id=1, source_target_pairs={{0,1},{1,2},{2,3},{3,4},{4,5},{5,6},{6,7},{7,8},{8,9},{9,10},{10,1... | collective-permute-start | bytes 3145736 | tf_op jit(solution)/shard_map/while/body/eval_jaxpr/ppermute | solution.py:16
  797.8 23.7 %collective-permute-start = (bf16[2,16,128,128]{3,2,1,0:T(8,128)(2,1)}, bf16[2,16,128,128]{3,2,1,0:T(8,128)(2,1)}, u32[]{:S(2)}, u32[]{:S(2)}) collective-permute-start(bf16[2,16,128,128]{3,2,1,0:T(8,128)(2,1)} %pad_maximum_fusion.4), channel_id=1, source_target_pairs={{0,1},{1,2},{2,3},{3,4},{4,5},{5,6},{6,7},{7,8},{8,9},{9,10},{10,1... | collective-permute-start | bytes 3145736 | tf_op jit(solution)/shard_map/while/body/eval_jaxpr/ppermute | solution.py:16
  829.3 22.8 %collective-permute-start = (bf16[2,16,128,128]{3,2,1,0:T(8,128)(2,1)}, bf16[2,16,128,128]{3,2,1,0:T(8,128)(2,1)}, u32[]{:S(2)}, u32[]{:S(2)}) collective-permute-start(bf16[2,16,128,128]{3,2,1,0:T(8,128)(2,1)} %pad_maximum_fusion.4), channel_id=1, source_target_pairs={{0,1},{1,2},{2,3},{3,4},{4,5},{5,6},{6,7},{7,8},{8,9},{9,10},{10,1... | collective-permute-start | bytes 3145736 | tf_op jit(solution)/shard_map/while/body/eval_jaxpr/ppermute | solution.py:16
  859.9 21.9 %collective-permute-start = (bf16[2,16,128,128]{3,2,1,0:T(8,128)(2,1)}, bf16[2,16,128,128]{3,2,1,0:T(8,128)(2,1)}, u32[]{:S(2)}, u32[]{:S(2)}) collective-permute-start(bf16[2,16,128,128]{3,2,1,0:T(8,128)(2,1)} %pad_maximum_fusion.4), channel_id=1, source_target_pairs={{0,1},{1,2},{2,3},{3,4},{4,5},{5,6},{6,7},{7,8},{8,9},{9,10},{10,1... | collective-permute-start | bytes 3145736 | tf_op jit(solution)/shard_map/while/body/eval_jaxpr/ppermute | solution.py:16
  889.6 20.9 %collective-permute-start = (bf16[2,16,128,128]{3,2,1,0:T(8,128)(2,1)}, bf16[2,16,128,128]{3,2,1,0:T(8,128)(2,1)}, u32[]{:S(2)}, u32[]{:S(2)}) collective-permute-start(bf16[2,16,128,128]{3,2,1,0:T(8,128)(2,1)} %pad_maximum_fusion.4), channel_id=1, source_target_pairs={{0,1},{1,2},{2,3},{3,4},{4,5},{5,6},{6,7},{7,8},{8,9},{9,10},{10,1... | collective-permute-start | bytes 3145736 | tf_op jit(solution)/shard_map/while/body/eval_jaxpr/ppermute | solution.py:16
  918.3 20.0 collective-permute-start
  946.1 19.1 collective-permute-start
  973.0 19.1 collective-permute-start
  999.9 19.1 collective-permute-start
  1026.8 19.1 collective-permute-start
  1048.9 2.9 copy-start.16
  1103.1 5.5 copy-start.4
  1109.8 2.6 copy-start.3
  1112.5 14.5 collective-permute-start.2
  1502.3 2.7 copy-start.6
  1516.1 2.7 copy-start.6
  1529.8 2.7 copy-start.6
  1551.5 28.5 %collective-permute-start.1 = (bf16[2,16,128,128]{3,2,1,0:T(8,128)(2,1)}, bf16[2,16,128,128]{3,2,1,0:T(8,128)(2,1)}, u32[]{:S(2)}, u32[]{:S(2)}) collective-permute-start(bf16[2,16,128,128]{3,2,1,0:T(8,128)(2,1)} %pad_maximum_fusion.5), channel_id=1, source_target_pairs={{0,1},{1,2},{2,3},{3,4},{4,5},{5,6},{6,7},{7,8},{8,9},{9,10},{10,1... | collective-permute-start | bytes 3145736 | tf_op jit(solution)/shard_map/while/body/eval_jaxpr/ppermute | solution.py:16
  1588.8 27.6 %collective-permute-start.1 = (bf16[2,16,128,128]{3,2,1,0:T(8,128)(2,1)}, bf16[2,16,128,128]{3,2,1,0:T(8,128)(2,1)}, u32[]{:S(2)}, u32[]{:S(2)}) collective-permute-start(bf16[2,16,128,128]{3,2,1,0:T(8,128)(2,1)} %pad_maximum_fusion.5), channel_id=1, source_target_pairs={{0,1},{1,2},{2,3},{3,4},{4,5},{5,6},{6,7},{7,8},{8,9},{9,10},{10,1... | collective-permute-start | bytes 3145736 | tf_op jit(solution)/shard_map/while/body/eval_jaxpr/ppermute | solution.py:16
  1625.2 26.7 %collective-permute-start.1 = (bf16[2,16,128,128]{3,2,1,0:T(8,128)(2,1)}, bf16[2,16,128,128]{3,2,1,0:T(8,128)(2,1)}, u32[]{:S(2)}, u32[]{:S(2)}) collective-permute-start(bf16[2,16,128,128]{3,2,1,0:T(8,128)(2,1)} %pad_maximum_fusion.5), channel_id=1, source_target_pairs={{0,1},{1,2},{2,3},{3,4},{4,5},{5,6},{6,7},{7,8},{8,9},{9,10},{10,1... | collective-permute-start | bytes 3145736 | tf_op jit(solution)/shard_map/while/body/eval_jaxpr/ppermute | solution.py:16
  1660.7 25.8 %collective-permute-start.1 = (bf16[2,16,128,128]{3,2,1,0:T(8,128)(2,1)}, bf16[2,16,128,128]{3,2,1,0:T(8,128)(2,1)}, u32[]{:S(2)}, u32[]{:S(2)}) collective-permute-start(bf16[2,16,128,128]{3,2,1,0:T(8,128)(2,1)} %pad_maximum_fusion.5), channel_id=1, source_target_pairs={{0,1},{1,2},{2,3},{3,4},{4,5},{5,6},{6,7},{7,8},{8,9},{9,10},{10,1... | collective-permute-start | bytes 3145736 | tf_op jit(solution)/shard_map/while/body/eval_jaxpr/ppermute | solution.py:16
  1695.3 24.8 %collective-permute-start.1 = (bf16[2,16,128,128]{3,2,1,0:T(8,128)(2,1)}, bf16[2,16,128,128]{3,2,1,0:T(8,128)(2,1)}, u32[]{:S(2)}, u32[]{:S(2)}) collective-permute-start(bf16[2,16,128,128]{3,2,1,0:T(8,128)(2,1)} %pad_maximum_fusion.5), channel_id=1, source_target_pairs={{0,1},{1,2},{2,3},{3,4},{4,5},{5,6},{6,7},{7,8},{8,9},{9,10},{10,1... | collective-permute-start | bytes 3145736 | tf_op jit(solution)/shard_map/while/body/eval_jaxpr/ppermute | solution.py:16
  1728.9 23.9 %collective-permute-start.1 = (bf16[2,16,128,128]{3,2,1,0:T(8,128)(2,1)}, bf16[2,16,128,128]{3,2,1,0:T(8,128)(2,1)}, u32[]{:S(2)}, u32[]{:S(2)}) collective-permute-start(bf16[2,16,128,128]{3,2,1,0:T(8,128)(2,1)} %pad_maximum_fusion.5), channel_id=1, source_target_pairs={{0,1},{1,2},{2,3},{3,4},{4,5},{5,6},{6,7},{7,8},{8,9},{9,10},{10,1... | collective-permute-start | bytes 3145736 | tf_op jit(solution)/shard_map/while/body/eval_jaxpr/ppermute | solution.py:16
  1761.6 23.0 %collective-permute-start.1 = (bf16[2,16,128,128]{3,2,1,0:T(8,128)(2,1)}, bf16[2,16,128,128]{3,2,1,0:T(8,128)(2,1)}, u32[]{:S(2)}, u32[]{:S(2)}) collective-permute-start(bf16[2,16,128,128]{3,2,1,0:T(8,128)(2,1)} %pad_maximum_fusion.5), channel_id=1, source_target_pairs={{0,1},{1,2},{2,3},{3,4},{4,5},{5,6},{6,7},{7,8},{8,9},{9,10},{10,1... | collective-permute-start | bytes 3145736 | tf_op jit(solution)/shard_map/while/body/eval_jaxpr/ppermute | solution.py:16
  1793.4 22.1 %collective-permute-start.1 = (bf16[2,16,128,128]{3,2,1,0:T(8,128)(2,1)}, bf16[2,16,128,128]{3,2,1,0:T(8,128)(2,1)}, u32[]{:S(2)}, u32[]{:S(2)}) collective-permute-start(bf16[2,16,128,128]{3,2,1,0:T(8,128)(2,1)} %pad_maximum_fusion.5), channel_id=1, source_target_pairs={{0,1},{1,2},{2,3},{3,4},{4,5},{5,6},{6,7},{7,8},{8,9},{9,10},{10,1... | collective-permute-start | bytes 3145736 | tf_op jit(solution)/shard_map/while/body/eval_jaxpr/ppermute | solution.py:16
  1824.3 21.1 %collective-permute-start.1 = (bf16[2,16,128,128]{3,2,1,0:T(8,128)(2,1)}, bf16[2,16,128,128]{3,2,1,0:T(8,128)(2,1)}, u32[]{:S(2)}, u32[]{:S(2)}) collective-permute-start(bf16[2,16,128,128]{3,2,1,0:T(8,128)(2,1)} %pad_maximum_fusion.5), channel_id=1, source_target_pairs={{0,1},{1,2},{2,3},{3,4},{4,5},{5,6},{6,7},{7,8},{8,9},{9,10},{10,1... | collective-permute-start | bytes 3145736 | tf_op jit(solution)/shard_map/while/body/eval_jaxpr/ppermute | solution.py:16
  1854.3 20.2 collective-permute-start.1
  1883.3 19.3 collective-permute-start.1
  1911.4 19.1 collective-permute-start.1
  1939.3 19.1 collective-permute-start.1
  1967.2 19.1 collective-permute-start.1
  1995.2 19.1 collective-permute-start.1
  2017.1 4.1 copy-start.10
  2070.0 3.9 copy-start.1
  (48 other events, 109.3 us)
Sparse Core Ops, SparseCore 0:
  9.5 156.2 all-gather.3
  1115.4 85.1 all-reduce.2
where the time goes:
time: 2100 us; the launch traced here: 2080 us
  other arithmetic  789 us (38%)
  waiting for transfers between devices  771 us (37%)
  matrix products  326 us (16%)
  local copies, waits for them, and re-layouts  74.7 us (4%)
  starting transfers between devices  57.7 us (3%)
  blocking collectives  24.4 us (1%)
  loops' own time  23.7 us (1%)
    another operation x5, other arithmetic, block_solve(): lax.linalg.triangular_solve(system, right_side, left_side=True, lower=Tru...  632 us
    ppermute x30, waiting for transfers between devices, from_behind(): return lax.ppermute(value, axis, pairs)  629 us
    all_gather x1, waiting for transfers between devices, shards(): lax.all_gather(w_qkv[0], 'seq', axis=0, tiled=True)  130 us
    select_n x30, other arithmetic, hop_once(): return jnp.where(position == 0, empty_map, passed)  87.6 us
    dot_general x30, matrix products, compose(): jnp.einsum('hij,hjk->hik', latter[0], earlier[0], precision=FULL_PRECISION)  74.3 us
    ppermute x30, starting transfers between devices, from_behind(): return lax.ppermute(value, axis, pairs)  57.6 us
    dot_general x30, matrix products, compose(): jnp.einsum('hij,hjk->hik', latter[0], earlier[1], precision=FULL_PRECISION)  54.3 us
  transfers between devices with their start and end apart: 33, of which 32 were waited for; matrix products, arithmetic and copies ran while one was open for 20% of the time, Pallas kernels for 0%

commit v1 on v0

--- a/solution.py
+++ b/solution.py
@@ -1,3 +1,4 @@
+import functools
 import jax
 import jax.numpy as jnp
 from jax import lax
@@ -8,6 +9,21 @@
 GROUP = 64
 TICKS = 2
 FULL_PRECISION = lax.Precision.HIGHEST
+
+
+def hold_vectors(frame, bus_axis, d0):
+    n_shards = jax.lax.axis_size(bus_axis)
+    inbox = []
+    dd = 0
+    while dd < frame.ndim:
+        inbox.append(n_shards if dd == d0 else 1)
+        dd = dd + 1
+    u1 = jnp.tile(frame, inbox)
+    next_value = jax.lax.all_to_all(u1, bus_axis, split_axis=d0, concat_axis=d0, tiled=True)
+    return next_value
+
+
+pipes_clear = functools.partial(hold_vectors, bus_axis="seq", d0=0)
 
 
 def from_behind(value, axis, by):
@@ -158,7 +174,7 @@
 
 def shards(residual, w_qkv, w_beta, beta_bias, norm_gain, out_gain, state_in, doc_start):
     weight_qkv, weight_beta = (
-        lax.all_gather(w_qkv[0], "seq", axis=0, tiled=True),
+        pipes_clear(w_qkv[0]),
         lax.all_gather(w_beta[0], "seq", axis=0, tiled=True),
     )
     seq_count = lax.axis_size("seq")

time: 2100 us -> 2340 us (1.11)
  blocking collectives: 24.4 us -> 389 us
  waiting for transfers between devices: 771 us -> 610 us
  local copies, waits for them, and re-layouts: 74.7 us -> 109 us
    all_gather x1, blocking collectives: 24.4 us -> 389 us  [shards(): lax.all_gather(w_beta[0], 'seq', axis=0, tiled=True)]
    all_gather x1 -> x0, waiting for transfers between devices: 130 us -> none  [shards(): lax.all_gather(w_qkv[0], 'seq', axis=0, tiled=True)]
    all_to_all x0 -> x1, local copies, waits for them, and re-layouts: none -> 31.3 us  [hold_vectors(): jax.lax.all_to_all(u1, bus_axis, split_axis=d0, concat_axis=d0, tiled=True)]
    ppermute x30, waiting for transfers between devices: 629 us -> 598 us  [from_behind(): return lax.ppermute(value, axis, pairs)]
  transfers between devices with their start and end apart: 33 -> 33, of which waited for: 32 -> 31; matrix products, arithmetic and copies ran while one was open for 20% -> 17% of each run, Pallas kernels for 0% -> 0%
where the time goes in v1:
time: 2340 us; the launch traced here: 2320 us
  other arithmetic  787 us (34%)
  waiting for transfers between devices  610 us (26%)
  blocking collectives  389 us (17%)
  matrix products  325 us (14%)
  local copies, waits for them, and re-layouts  109 us (5%)
  starting transfers between devices  65.5 us (3%)
  loops' own time  24 us (1%)
    another operation x5, other arithmetic, block_solve(): lax.linalg.triangular_solve(system, right_side, left_side=True, lower=Tru...  632 us
    ppermute x30, waiting for transfers between devices, from_behind(): return lax.ppermute(value, axis, pairs)  598 us
    all_gather x1, blocking collectives, shards(): lax.all_gather(w_beta[0], 'seq', axis=0, tiled=True)  389 us
    select_n x30, other arithmetic, hop_once(): return jnp.where(position == 0, empty_map, passed)  87.8 us
    dot_general x30, matrix products, compose(): jnp.einsum('hij,hjk->hik', latter[0], earlier[0], precision=FULL_PRECISION)  74.3 us
    ppermute x30, starting transfers between devices, from_behind(): return lax.ppermute(value, axis, pairs)  57.3 us
    dot_general x30, matrix products, compose(): jnp.einsum('hij,hjk->hik', latter[0], earlier[1], precision=FULL_PRECISION)  54.3 us
  transfers between devices with their start and end apart: 33, of which 31 were waited for; matrix products, arithmetic and copies ran while one was open for 17% of the time, Pallas kernels for 0%

profile of v1, /device:TPU:34, one launch (start us, length us, event | category | flops | bytes accessed | tf_op | source)
XLA Modules:
  0.0 2323.5 jit_solution(5422136559978266999)
XLA Ops:
  8.5 8.8 tile.9
  17.3 8.2 all-to-all-start
  25.6 388.5 %all-gather = bf16[1,2048,16]{1,2,0:T(8,128)(2,1)S(1)} all-gather(bf16[1,128,16]{1,2,0:T(8,128)(2,1)S(1)} %copy-done.18), channel_id=2, replica_groups=mesh['section'=8,'seq'=16] {'seq'}, dimensions={1}, use_global_device_ids=true | all-gather | bytes 69632 | tf_op jit(solution)/shard_map/all_gather | solution.py:178
  418.1 31.3 %copy.60 = bf16[16,128,6144]{2,1,0:T(8,128)(2,1)} copy(bf16[16,128,6144]{1,2,0:T(8,128)(2,1)} %all-to-all-done) | data formatting | bytes 50331648 | tf_op jit(solution)/shard_map/all_to_all | solution.py:22
  449.4 31.7 %copy.61 = bf16[6144,2048]{1,0:T(8,128)(2,1)} copy(bf16[6144,2048]{0,1:T(8,128)(2,1)} %bitcast.352) | data formatting | bytes 50331648 | tf_op jit(solution)/shard_map/dot_general | solution.py:71
  481.2 11.4 fusion.151
  503.4 316.0 %custom-call.6 = f32[4,16,1,64,64]{3,4,2,1,0:T(8,128)} custom-call(f32[4,16,1,64,64]{4,3,2,1,0:T(8,128)} %add_bitcast_fusion.1), custom_call_target="InvertDiagBlocksLowerTriangular" | custom-call | tf_op jit(solution)/shard_map/triangular_solve/custom-call.1 | solution.py:58
  819.4 6.6 fusion.110
  828.8 41.9 %while.80 = (s32[]{:T(128)}, f32[16,128,128]{2,1,0:T(8,128)S(1)}, f32[16,128,128]{2,1,0:T(8,128)S(1)}, s32[4]{0:T(128)S(1)}, s32[]{:T(128)}, /*index=5*/f32[4,16...) while((s32[]{:T(128)}, f32[16,128,128]{2,1,0:T(8,128)S(1)}, ...), condition=%wide.region_3.5_spmd.clone, body=%wide.region_2.4_spmd.clone.sunk | while | flops 807534592 | bytes 19400364 | solution.py:149
  870.8 433.5 %while.76 = (s32[]{:T(128)}, f32[2,16,128,128]{3,2,1,0:T(8,128)}, pred[]{:T(512)}, f32[16,128,128]{2,1,0:T(8,128)S(1)}, f32[16,128,128]{2,1,0:T(8,128)S(1)}, /*index=5*/f32[2,16,128,128]{3,2,1,0:T(8,128)}, s32[]{:T(128)}) while((s32[]{:T(128)}, f32[2,16,128,128]{3,2,1,0:T(8,128)}, pred[]{:T(512)}, f32[16,128,128]{2,1,0:T(8,128)S(1)}, ...), condition=%wide.region_5.7_spmd, body=%wide.region_4.6_spmd.sunk | while | flops 807665664 | bytes 26214544 | solution.py:203
  877.5 22.0 collective-permute-done
  909.2 21.0 collective-permute-done
  939.9 20.1 collective-permute-done
  969.8 19.2 collective-permute-done
  998.6 18.3 collective-permute-done
  1026.6 17.3 collective-permute-done
  1053.7 17.2 collective-permute-done
  1080.6 17.2 collective-permute-done
  1107.5 17.2 collective-permute-done
  1134.4 18.1 collective-permute-done
  1162.2 19.1 collective-permute-done
  1191.0 20.2 collective-permute-done
  1221.0 21.3 collective-permute-done
  1252.0 22.4 collective-permute-done
  1284.1 17.2 collective-permute-done
  1310.4 48.2 %while.78 = (s32[]{:T(128)}, f32[16,128,128]{2,1,0:T(8,128)S(1)}, f32[4,16,64,128]{3,2,1,0:T(8,128)}, s32[4]{0:T(128)S(1)}, s32[]{:T(128)}, /*index=5*/f32[4,16,...) while((s32[]{:T(128)}, f32[16,128,128]{2,1,0:T(8,128)S(1)}, ...), condition=%wide.region_8.10_spmd.clone, body=%wide.region_7.9_spmd.clone.sunk | while | flops 806690816 | bytes 19451036 | solution.py:116
  1370.8 11.7 collective-permute-done.2
  1384.1 11.9 fusion.154
  1409.7 316.0 %custom-call.7 = f32[4,16,1,64,64]{3,4,2,1,0:T(8,128)} custom-call(f32[4,16,1,64,64]{4,3,2,1,0:T(8,128)} %add_bitcast_fusion), custom_call_target="InvertDiagBlocksLowerTriangular" | custom-call | tf_op jit(solution)/shard_map/triangular_solve/custom-call.1 | solution.py:58
  1725.7 6.6 fusion.114
  1735.0 54.6 %while.81 = (s32[]{:T(128)}, f32[16,128,128]{2,1,0:T(8,128)S(1)}, f32[16,128,128]{2,1,0:T(8,128)}, s32[4]{0:T(128)S(1)}, s32[]{:T(128)}, /*index=5*/f32[4,16,64,...) while((s32[]{:T(128)}, f32[16,128,128]{2,1,0:T(8,128)S(1)}, ...), condition=%wide.region_13.15_spmd.clone, body=%wide.region_12.14_spmd.clone.sunk | while | flops 807534592 | bytes 19401408 | solution.py:149
  1792.7 471.6 %while.77 = (s32[]{:T(128)}, f32[2,16,128,128]{3,2,1,0:T(8,128)}, pred[]{:T(512)}, f32[16,128,128]{2,1,0:T(8,128)S(1)}, f32[16,128,128]{2,1,0:T(8,128)}, /*index=5*/f32[2,16,128,128]{3,2,1,0:T(8,128)S(1)}, s32[]{:T(128)}) while((s32[]{:T(128)}, f32[2,16,128,128]{3,2,1,0:T(8,128)}, pred[]{:T(512)}, f32[16,128,128]{2,1,0:T(8,128)S(1)}, ...), condition=%wide.region_15.17_spmd, body=%wide.region_14.16_spmd.sunk | while | flops 807665664 | bytes 22020240 | solution.py:203
  1800.6 26.6 %collective-permute-done.1 = bf16[2,16,128,128]{3,2,1,0:T(8,128)(2,1)} collective-permute-done((bf16[2,16,128,128]{3,2,1,0:T(8,128)(2,1)}, bf16[2,16,128,128]{3,2,1,0:T(8,128)(2,1)}, u32[]{:S(2)}, u32[]{:S(2)}) %collective-permute-start.1) | collective-permute-done | bytes 1048608 | tf_op jit(solution)/shard_map/while/body/eval_jaxpr/ppermute | solution.py:32
  1837.9 25.7 %collective-permute-done.1 = bf16[2,16,128,128]{3,2,1,0:T(8,128)(2,1)} collective-permute-done((bf16[2,16,128,128]{3,2,1,0:T(8,128)(2,1)}, bf16[2,16,128,128]{3,2,1,0:T(8,128)(2,1)}, u32[]{:S(2)}, u32[]{:S(2)}) %collective-permute-start.1) | collective-permute-done | bytes 1048608 | tf_op jit(solution)/shard_map/while/body/eval_jaxpr/ppermute | solution.py:32
  1874.3 24.8 %collective-permute-done.1 = bf16[2,16,128,128]{3,2,1,0:T(8,128)(2,1)} collective-permute-done((bf16[2,16,128,128]{3,2,1,0:T(8,128)(2,1)}, bf16[2,16,128,128]{3,2,1,0:T(8,128)(2,1)}, u32[]{:S(2)}, u32[]{:S(2)}) %collective-permute-start.1) | collective-permute-done | bytes 1048608 | tf_op jit(solution)/shard_map/while/body/eval_jaxpr/ppermute | solution.py:32
  1909.8 23.8 %collective-permute-done.1 = bf16[2,16,128,128]{3,2,1,0:T(8,128)(2,1)} collective-permute-done((bf16[2,16,128,128]{3,2,1,0:T(8,128)(2,1)}, bf16[2,16,128,128]{3,2,1,0:T(8,128)(2,1)}, u32[]{:S(2)}, u32[]{:S(2)}) %collective-permute-start.1) | collective-permute-done | bytes 1048608 | tf_op jit(solution)/shard_map/while/body/eval_jaxpr/ppermute | solution.py:32
  1944.3 22.9 collective-permute-done.1
  1978.0 22.0 collective-permute-done.1
  2010.7 21.1 collective-permute-done.1
  2042.5 20.1 collective-permute-done.1
  2073.4 19.2 collective-permute-done.1
  2103.3 18.3 collective-permute-done.1
  2132.4 17.4 collective-permute-done.1
  2160.5 17.2 collective-permute-done.1
  2188.4 17.2 collective-permute-done.1
  2216.3 17.2 collective-permute-done.1
  2244.2 17.2 collective-permute-done.1
  2268.4 39.6 %while.79 = (s32[]{:T(128)}, f32[16,128,128]{2,1,0:T(8,128)S(1)}, f32[4,16,64,128]{3,2,1,0:T(8,128)}, s32[4]{0:T(128)S(1)}, s32[]{:T(128)}, /*index=5*/f32[4,16,...) while((s32[]{:T(128)}, f32[16,128,128]{2,1,0:T(8,128)S(1)}, ...), condition=%wide.region_19.21_spmd.clone, body=%wide.region_18.20_spmd.clone.sunk | while | flops 806690816 | bytes 19451036 | solution.py:116
  (451 shorter events, 538.1 us)
Async XLA Ops:
  6.5 1297.7 %copy-start = (f32[1,16,128,128]{3,2,1,0:T(8,128)S(1)}, f32[1,16,128,128]{3,2,1,0:T(8,128)}, u32[]{:S(2)}) copy-start(f32[1,16,128,128]{3,2,1,0:T(8,128)} %param.28) | copy-start | bytes 3145732
  17.3 8.3 copy-start.18
  17.3 396.8 %copy-start.16 = (bf16[1,256,2048]{2,1,0:T(8,128)(2,1)S(1)}, bf16[1,256,2048]{2,1,0:T(8,128)(2,1)}, u32[]{:S(2)}) copy-start(bf16[1,256,2048]{2,1,0:T(8,128)(2,1)} %param.22) | copy-start | bytes 3145732
  17.3 397.1 %copy-start.21 = (f32[1,2048]{1,0:T(1,128)S(1)}, f32[1,2048]{1,0:T(1,128)}, u32[]{:S(2)}) copy-start(f32[1,2048]{1,0:T(1,128)} %param.26) | copy-start | bytes 24580
  17.3 397.1 %copy-start.22 = (f32[1,16]{1,0:T(1,128)S(1)}, f32[1,16]{1,0:T(1,128)}, u32[]{:S(2)}) copy-start(f32[1,16]{1,0:T(1,128)} %param.25) | copy-start | bytes 196
  17.3 400.8 %all-to-all-start = ((bf16[16,128,6144]{1,2,0:T(8,128)(2,1)}), bf16[16,128,6144]{1,2,0:T(8,128)(2,1)}, u32[]{:S(2)}, u32[]{:S(2)}) async-start(bf16[16,128,6144]{1,2,0:T(8,128)(2,1)} %tile.9), calls=%async_computation | async-start | bytes 50331648 | tf_op jit(solution)/shard_map/all_to_all | solution.py:22
  25.5 1767.2 %all-reduce.3.cloned.1.call-start = ((), (), s32[]{:S(2)}) async-start(), calls=%async_computation.1 | async-start | bytes 1048576 | tf_op jit(solution)/shard_map/psum | solution.py:37
  415.4 2.6 copy-start.20
  870.8 2.5 copy-start.9
  875.6 23.9 %collective-permute-start = (bf16[2,16,128,128]{3,2,1,0:T(8,128)(2,1)}, bf16[2,16,128,128]{3,2,1,0:T(8,128)(2,1)}, u32[]{:S(2)}, u32[]{:S(2)}) collective-permute-start(bf16[2,16,128,128]{3,2,1,0:T(8,128)(2,1)} %pad_maximum_fusion.4), channel_id=1, source_target_pairs={{0,1},{1,2},{2,3},{3,4},{4,5},{5,6},{6,7},{7,8},{8,9},{9,10},{10,1... | collective-permute-start | bytes 3145736 | tf_op jit(solution)/shard_map/while/body/eval_jaxpr/ppermute | solution.py:32
  907.3 22.9 collective-permute-start
  938.0 22.0 collective-permute-start
  967.8 21.1 collective-permute-start
  996.7 20.2 collective-permute-start
  1024.7 19.3 collective-permute-start
  1051.8 19.1 collective-permute-start
  1078.7 19.1 collective-permute-start
  1105.6 19.1 collective-permute-start
  1132.5 20.0 collective-permute-start
  1160.2 21.1 collective-permute-start
  1189.1 22.1 collective-permute-start
  1219.0 23.2 collective-permute-start
  1250.0 24.3 %collective-permute-start = (bf16[2,16,128,128]{3,2,1,0:T(8,128)(2,1)}, bf16[2,16,128,128]{3,2,1,0:T(8,128)(2,1)}, u32[]{:S(2)}, u32[]{:S(2)}) collective-permute-start(bf16[2,16,128,128]{3,2,1,0:T(8,128)(2,1)} %pad_maximum_fusion.4), channel_id=1, source_target_pairs={{0,1},{1,2},{2,3},{3,4},{4,5},{5,6},{6,7},{7,8},{8,9},{9,10},{10,1... | collective-permute-start | bytes 3145736 | tf_op jit(solution)/shard_map/while/body/eval_jaxpr/ppermute | solution.py:32
  1282.1 19.1 collective-permute-start
  1304.2 2.9 copy-start.15
  1358.6 5.5 copy-start.4
  1365.4 2.7 copy-start.3
  1368.0 14.5 collective-permute-start.2
  1750.4 2.7 copy-start.6
  1764.1 2.7 copy-start.6
  1777.8 2.7 copy-start.6
  1798.6 28.5 %collective-permute-start.1 = (bf16[2,16,128,128]{3,2,1,0:T(8,128)(2,1)}, bf16[2,16,128,128]{3,2,1,0:T(8,128)(2,1)}, u32[]{:S(2)}, u32[]{:S(2)}) collective-permute-start(bf16[2,16,128,128]{3,2,1,0:T(8,128)(2,1)} %pad_maximum_fusion.5), channel_id=1, source_target_pairs={{0,1},{1,2},{2,3},{3,4},{4,5},{5,6},{6,7},{7,8},{8,9},{9,10},{10,1... | collective-permute-start | bytes 3145736 | tf_op jit(solution)/shard_map/while/body/eval_jaxpr/ppermute | solution.py:32
  1836.0 27.6 %collective-permute-start.1 = (bf16[2,16,128,128]{3,2,1,0:T(8,128)(2,1)}, bf16[2,16,128,128]{3,2,1,0:T(8,128)(2,1)}, u32[]{:S(2)}, u32[]{:S(2)}) collective-permute-start(bf16[2,16,128,128]{3,2,1,0:T(8,128)(2,1)} %pad_maximum_fusion.5), channel_id=1, source_target_pairs={{0,1},{1,2},{2,3},{3,4},{4,5},{5,6},{6,7},{7,8},{8,9},{9,10},{10,1... | collective-permute-start | bytes 3145736 | tf_op jit(solution)/shard_map/while/body/eval_jaxpr/ppermute | solution.py:32
  1872.4 26.7 %collective-permute-start.1 = (bf16[2,16,128,128]{3,2,1,0:T(8,128)(2,1)}, bf16[2,16,128,128]{3,2,1,0:T(8,128)(2,1)}, u32[]{:S(2)}, u32[]{:S(2)}) collective-permute-start(bf16[2,16,128,128]{3,2,1,0:T(8,128)(2,1)} %pad_maximum_fusion.5), channel_id=1, source_target_pairs={{0,1},{1,2},{2,3},{3,4},{4,5},{5,6},{6,7},{7,8},{8,9},{9,10},{10,1... | collective-permute-start | bytes 3145736 | tf_op jit(solution)/shard_map/while/body/eval_jaxpr/ppermute | solution.py:32
  1907.9 25.8 %collective-permute-start.1 = (bf16[2,16,128,128]{3,2,1,0:T(8,128)(2,1)}, bf16[2,16,128,128]{3,2,1,0:T(8,128)(2,1)}, u32[]{:S(2)}, u32[]{:S(2)}) collective-permute-start(bf16[2,16,128,128]{3,2,1,0:T(8,128)(2,1)} %pad_maximum_fusion.5), channel_id=1, source_target_pairs={{0,1},{1,2},{2,3},{3,4},{4,5},{5,6},{6,7},{7,8},{8,9},{9,10},{10,1... | collective-permute-start | bytes 3145736 | tf_op jit(solution)/shard_map/while/body/eval_jaxpr/ppermute | solution.py:32
  1942.4 24.8 %collective-permute-start.1 = (bf16[2,16,128,128]{3,2,1,0:T(8,128)(2,1)}, bf16[2,16,128,128]{3,2,1,0:T(8,128)(2,1)}, u32[]{:S(2)}, u32[]{:S(2)}) collective-permute-start(bf16[2,16,128,128]{3,2,1,0:T(8,128)(2,1)} %pad_maximum_fusion.5), channel_id=1, source_target_pairs={{0,1},{1,2},{2,3},{3,4},{4,5},{5,6},{6,7},{7,8},{8,9},{9,10},{10,1... | collective-permute-start | bytes 3145736 | tf_op jit(solution)/shard_map/while/body/eval_jaxpr/ppermute | solution.py:32
  1976.1 23.9 %collective-permute-start.1 = (bf16[2,16,128,128]{3,2,1,0:T(8,128)(2,1)}, bf16[2,16,128,128]{3,2,1,0:T(8,128)(2,1)}, u32[]{:S(2)}, u32[]{:S(2)}) collective-permute-start(bf16[2,16,128,128]{3,2,1,0:T(8,128)(2,1)} %pad_maximum_fusion.5), channel_id=1, source_target_pairs={{0,1},{1,2},{2,3},{3,4},{4,5},{5,6},{6,7},{7,8},{8,9},{9,10},{10,1... | collective-permute-start | bytes 3145736 | tf_op jit(solution)/shard_map/while/body/eval_jaxpr/ppermute | solution.py:32
  2008.8 23.0 collective-permute-start.1
  2040.6 22.1 collective-permute-start.1
  2071.5 21.1 collective-permute-start.1
  2101.4 20.2 collective-permute-start.1
  2130.5 19.3 collective-permute-start.1
  2158.6 19.1 collective-permute-start.1
  2186.5 19.1 collective-permute-start.1
  2214.4 19.1 collective-permute-start.1
  2242.3 19.1 collective-permute-start.1
  2264.3 4.1 copy-start.10
  2312.3 3.9 copy-start.1
  (51 other events, 117.5 us)
Sparse Core Ops, SparseCore 0:
  1371.0 84.1 all-reduce.2
